TPU v7x, 256 devices: a whole 4x4x8 slice. The times are simulated.
256 devices in a mesh: line: 8 (over z_lo, core), bus: 32 (over y, x, z_hi).
Axes of the slice: x: 4, y: 4, z: 8 (z_hi: 2, z_lo: 4; z = z_hi * 4 + z_lo), core: 2. Of those that a mesh axis runs over, the one named last changes fastest.
Arguments:
- injections: float32 [64, 69632], P(None, 'bus'), may hold values from -6 to 6
- transfer_factors: float32 [4096, 69632], P('line', 'bus'), may hold values from -0.0234375 to 0.0234375
- outage_factors: float32 [4096, 8192], P('line', 'bus'), may hold values from -1 to 1
- outage_line: int32 [8192], P('bus'), may hold values from 0 to 4095
- limit_table: int32 [4, 4096], P(None, 'line'), may hold values from 1 to 4
- scenario_tier: int32 [64], replicated, may hold values from 0 to 3
Outputs:
- injection_grad: float32 [64, 69632], P('line', 'bus')
- mean_penalty: float32 [64], replicated
All inputs are finite; a program needn't handle non-finite values.
Results may differ from a plain program's by a relative error of at most 0.0003.
Values sent between devices are 32-bit elements; how exact they have to be, the bound alone decides.
A program may use at most 64 MiB of HBM per device.

v0:
```python
import math
import jax
import jax.numpy as jnp
from jax import lax
from jax.sharding import PartitionSpec as P

LINES = 4096
OUTAGES = 8192


def body(injections, transfer_factors, outage_factors, outage_line, limit_table, scenario_tier):
    scenarios = injections.shape[0]
    line_rows = transfer_factors.shape[0]
    outage_cols = outage_factors.shape[1]
    partial_flows = jnp.dot(
        injections,
        transfer_factors.T,
        precision=lax.Precision.HIGHEST,
        preferred_element_type=jnp.float32,
    )
    line_flows = lax.psum(partial_flows, "bus")
    line_start = lax.axis_index("line") * line_rows
    local_index = outage_line - line_start
    selector = (local_index[None, :] == jnp.arange(line_rows, dtype=jnp.int32)[:, None]).astype(
        jnp.float32
    )
    every_flow = lax.all_gather(line_flows, "line", axis=1, tiled=True)
    outage_flows = jnp.take(every_flow, outage_line, axis=1)
    tier_onehot = (
        scenario_tier[:, None] == jnp.arange(limit_table.shape[0], dtype=jnp.int32)[None, :]
    ).astype(jnp.float32)
    limits = 0.4 * jnp.dot(
        tier_onehot,
        limit_table.astype(jnp.float32),
        precision=lax.Precision.HIGHEST,
        preferred_element_type=jnp.float32,
    )
    block_rows = math.gcd(scenarios, 16)
    num_blocks = scenarios // block_rows

    def one_block(values):
        flow_block, outage_block, limit_block = values
        post = flow_block[:, :, None] + outage_factors[None, :, :] * outage_block[:, None, :]
        excess = jnp.maximum(jnp.abs(post) - limit_block[:, :, None], 0.0)
        weight = 2.0 * excess * jnp.sign(post) / OUTAGES
        return (
            jnp.sum(excess * excess, axis=(1, 2)),
            jnp.sum(weight, axis=2),
            jnp.sum(weight * outage_factors[None, :, :], axis=1),
        )

    penalty, direct, back_part = lax.map(
        one_block,
        (
            line_flows.reshape(num_blocks, block_rows, line_rows),
            outage_flows.reshape(num_blocks, block_rows, outage_cols),
            limits.reshape(num_blocks, block_rows, line_rows),
        ),
    )
    penalty = penalty.reshape(scenarios)
    direct = direct.reshape(scenarios, line_rows)
    back_part = back_part.reshape(scenarios, outage_cols)
    back = lax.psum(back_part, "line")
    carried = jnp.dot(
        back, selector.T, precision=lax.Precision.HIGHEST, preferred_element_type=jnp.float32
    )
    flow_grad, penalty_sum = lax.psum((direct + carried, penalty), "bus")
    total_penalty = lax.psum(penalty, ("line", "bus"))
    mean_penalty = total_penalty / (LINES * OUTAGES)
    injection_grad = lax.psum_scatter(
        jnp.dot(
            flow_grad,
            transfer_factors,
            precision=lax.Precision.HIGHEST,
            preferred_element_type=jnp.float32,
        ),
        "line",
        scatter_dimension=0,
        tiled=True,
    )
    return (injection_grad, mean_penalty)


def solution(mesh):
    return jax.shard_map(
        body,
        mesh=mesh,
        in_specs=(
            P(None, "bus"),
            P("line", "bus"),
            P("line", "bus"),
            P("bus"),
            P(None, "line"),
            P(),
        ),
        out_specs=(P("line", "bus"), P()),
        check_vma=False,
    )
```

profile of v0, /device:TPU:1, one launch (start us, length us, event | category | flops | bytes accessed | tf_op | source)
XLA Modules:
  0.0 1058.1 jit_solution(12316503134355533745)
XLA Ops:
  7.2 0.0 copy-start
  7.2 0.0 copy-start.3
  7.2 0.0 copy-start.2
  7.2 0.0 copy-start.4
  7.2 0.0 copy-start.1
  7.2 0.0 all-reduce.6.cloned.1.call-start
  7.3 1.0 copy-done
  8.2 7.2 fusion.3
  15.5 0.0 all-reduce.6.cloned.1.call-update
  15.5 0.0 all-gather.2.cloned.1.call-start
  15.5 387.3 %all-reduce.6.cloned.1.call-done = f32[64,512]{1,0:T(8,128)} async-done(((f32[64,512]{1,0:T(8,128)}), f32[64,512]{1,0:T(8,128)}) %all-reduce.6.cloned.1.call-update) | async-done | bytes 131088 | tf_op jit(solution)/shard_map/psum | solution.py:21
  402.9 0.0 all-gather.2.cloned.1.call-update
  402.9 0.0 all-reduce.8.cloned.1.call-start
  403.0 0.0 copy-done.3
  403.0 0.0 copy-done.2
  403.0 0.0 copy-done.4
  403.0 0.3 convolution_multiply_fusion
  403.3 49.7 %all-gather.2.cloned.1.call-done = f32[64,4096]{1,0:T(8,128)} async-done(((f32[64,512]{1,0:T(8,128)}), f32[64,4096]{1,0:T(8,128)}) %all-gather.2.cloned.1.call-update) | async-done | bytes 1048592 | tf_op jit(solution)/shard_map/all_gather | solution.py:27
  453.0 1.8 copy.14
  454.8 0.7 gather_fusion
  455.6 0.1 copy.15
  455.7 0.0 copy-done.1
  455.7 40.5 %while.14 = (s32[]{:T(128)}, f32[4,16]{1,0:T(4,128)S(1)}, f32[4,16,512]{2,1,0:T(8,128)}, f32[4,16,256]{2,1,0:T(8,128)}, f32[4,16,512]{2,1,0:T(8,128)}, /*index=5...) while((s32[]{:T(128)}, f32[4,16]{1,0:T(4,128)S(1)}, ...), condition=%wide.region_5.6_spmd, body=%wide.region_1.5_spmd.sunk | while | flops 29478896 | bytes 2491697 | solution.py:52
  455.7 0.8 dynamic-slice_bitcast_fusion.5
  456.5 8.0 multiply_reduce_fusion.4
  464.5 0.6 bitcast_dynamic-update-slice_fusion.4
  465.2 0.6 bitcast_dynamic-update-slice_fusion.5
  465.8 0.8 dynamic-slice_bitcast_fusion.5
  466.6 8.0 multiply_reduce_fusion.4
  474.7 0.6 bitcast_dynamic-update-slice_fusion.4
  475.3 0.6 bitcast_dynamic-update-slice_fusion.5
  475.9 0.8 dynamic-slice_bitcast_fusion.5
  476.7 8.0 multiply_reduce_fusion.4
  484.8 0.6 bitcast_dynamic-update-slice_fusion.4
  485.4 0.6 bitcast_dynamic-update-slice_fusion.5
  486.0 0.8 dynamic-slice_bitcast_fusion.5
  486.8 8.0 multiply_reduce_fusion.4
  494.9 0.6 bitcast_dynamic-update-slice_fusion.4
  495.5 0.6 bitcast_dynamic-update-slice_fusion.5
  496.1 0.0 copy-start.5
  496.1 0.0 all-reduce.8.cloned.1.call-update
  496.2 0.0 all-reduce.10.cloned.1.call-start
  496.2 68.3 %all-reduce.8.cloned.1.call-done = f32[64,256]{1,0:T(8,128)} async-done(((f32[64,256]{1,0:T(8,128)}), f32[64,256]{1,0:T(8,128)}) %all-reduce.8.cloned.1.call-update) | async-done | bytes 65552 | tf_op jit(solution)/shard_map/psum | solution.py:63
  564.5 2.0 convolution_add_fusion
  566.5 0.0 all-reduce.10.cloned.1.call-update
  566.5 0.0 all-reduce.12.cloned.1.call-start
  566.6 385.1 %all-reduce.10.cloned.1.call-done = f32[64,512]{1,0:T(8,128)} async-done(((f32[64,512]{1,0:T(8,128)}), f32[64,512]{1,0:T(8,128)}) %all-reduce.10.cloned.1.call-update) | async-done | bytes 131088 | tf_op jit(solution)/shard_map/psum | solution.py:67
  951.6 5.9 fusion.4
  957.6 0.0 all-reduce.12.cloned.1.call-update
  957.6 0.0 copy-done.5
  957.6 0.6 dynamic-slice
  958.8 0.1 reshape.44
  958.9 90.6 %psum.31 = f32[64]{0:T(128)S(1)} all-reduce(f32[64]{0:T(128)S(1)} %reshape.44), channel_id=1, replica_groups=mesh['line'=8,'bus'=32] {'line','bus'}, use_global_device_ids=true, to_apply=%region_9.10 | all-reduce | flops 64 | bytes 512 | tf_op jit(solution)/shard_map/psum | solution.py:68
  1049.5 0.5 broadcast_multiply_fusion.1
  1050.0 0.0 all-reduce.12.cloned.1.call-done
  1050.0 1.5 constant_dynamic-slice_fusion
  (19 shorter events, 0.3 us)
Async XLA Ops:
  7.2 1.1 copy-start
  7.2 395.8 %copy-start.3 = (s32[256]{0:T(256)S(1)}, s32[256]{0:T(256)}, u32[]{:S(2)}) copy-start(s32[256]{0:T(256)} %param.11) | copy-start | bytes 3076
  7.2 395.8 %copy-start.2 = (s32[4,512]{1,0:T(4,128)S(1)}, s32[4,512]{1,0:T(4,128)}, u32[]{:S(2)}) copy-start(s32[4,512]{1,0:T(4,128)} %param.12) | copy-start | bytes 24580
  7.2 395.8 %copy-start.4 = (s32[64]{0:T(128)S(1)}, s32[64]{0:T(128)}, u32[]{:S(2)}) copy-start(s32[64]{0:T(128)} %param.13) | copy-start | bytes 772
  7.2 448.4 %copy-start.1 = (f32[512,256]{1,0:T(8,128)S(1)}, f32[512,256]{1,0:T(8,128)}, u32[]{:S(2)}) copy-start(f32[512,256]{1,0:T(8,128)} %param.10) | copy-start | bytes 1572868
  7.2 395.6 %all-reduce.6.cloned.1.call-start = ((), (), s32[]{:S(2)}) async-start(), calls=%async_computation | async-start | bytes 262144 | tf_op jit(solution)/shard_map/psum | solution.py:21
  15.5 437.5 %all-gather.2.cloned.1.call-start = ((), (), s32[]{:S(2)}) async-start(), calls=%async_computation.1 | async-start | bytes 1179648 | tf_op jit(solution)/shard_map/all_gather | solution.py:27
  402.9 161.6 %all-reduce.8.cloned.1.call-start = ((), (), s32[]{:S(2)}) async-start(), calls=%async_computation.2 | async-start | bytes 131072 | tf_op jit(solution)/shard_map/psum | solution.py:63
  496.1 461.5 %copy-start.5 = (u32[256]{0:T(256)S(1)}, u32[256]{0:T(256)}, u32[]{:S(2)}) copy-start(u32[256]{0:T(256)} %constant.60) | copy-start | bytes 3076
  496.2 455.5 %all-reduce.10.cloned.1.call-start = ((), (), s32[]{:S(2)}) async-start(), calls=%async_computation.3 | async-start | bytes 262144 | tf_op jit(solution)/shard_map/psum | solution.py:67
  566.5 483.5 %all-reduce.12.cloned.1.call-start = ((), (), s32[]{:S(2)}) async-start(), calls=%async_computation.4 | async-start | bytes 1114112
Sparse Core Ops, SparseCore 0:
  15.6 387.1 all-reduce.5
  404.8 48.1 all-gather.1
  496.3 68.2 all-reduce.7
  567.0 384.6 all-reduce.9
  957.7 82.9 all-reduce.11
where the time goes:
time: 1060 us
  waiting for transfers between devices  890 us (84%)
  blocking collectives  90.6 us (9%)
  other arithmetic  32.9 us (3%)
  matrix products  15.4 us (1%)
  between operations  14.6 us (1%)
  local copies, waits for them, and re-layouts  13.9 us (1%)
    psum x1, waiting for transfers between devices, body(): line_flows = lax.psum(partial_flows, 'bus')  387 us
    psum x1, waiting for transfers between devices, body(): flow_grad, penalty_sum = lax.psum((direct + carried, penalty), 'bus')  385 us
    psum x1, blocking collectives, body(): total_penalty = lax.psum(penalty, ('line', 'bus'))  90.6 us
    psum x1, waiting for transfers between devices, body(): back = lax.psum(back_part, 'line')  68.3 us
    all_gather x1, waiting for transfers between devices, body(): every_flow = lax.all_gather(line_flows, 'line', axis=1, tiled=True)  49.7 us
    reduce_sum x4, other arithmetic, one_block(): jnp.sum(weight * outage_factors[None, :, :], axis=1)  32.2 us
  transfers between devices with their start and end apart: 5, of which 4 were waited for; matrix products, arithmetic and copies ran while one was open for 0% of the time, Pallas kernels for 0%

commit v1 on v0

--- a/solution.py
+++ b/solution.py
@@ -65,7 +65,7 @@
         back, selector.T, precision=lax.Precision.HIGHEST, preferred_element_type=jnp.float32
     )
     flow_grad, penalty_sum = lax.psum((direct + carried, penalty), "bus")
-    total_penalty = lax.psum(penalty, ("line", "bus"))
+    total_penalty = lax.psum(lax.psum(penalty, "bus"), "line")
     mean_penalty = total_penalty / (LINES * OUTAGES)
     injection_grad = lax.psum_scatter(
         jnp.dot(

time: 1060 us -> 1110 us (1.047)
  blocking collectives: 90.6 us -> 145 us
    psum x1 -> x2, blocking collectives: 90.6 us -> 145 us  [body(): total_penalty = lax.psum(lax.psum(penalty, 'bus'), 'line')]
where the time goes in v1:
time: 1110 us
  waiting for transfers between devices  890 us (80%)
  blocking collectives  145 us (13%)
  other arithmetic  32.9 us (3%)
  matrix products  15.4 us (1%)
  between operations  14.6 us (1%)
  local copies, waits for them, and re-layouts  13.9 us (1%)
    psum x1, waiting for transfers between devices, body(): line_flows = lax.psum(partial_flows, 'bus')  387 us
    psum x1, waiting for transfers between devices, body(): flow_grad, penalty_sum = lax.psum((direct + carried, penalty), 'bus')  385 us
    psum x2, blocking collectives, body(): total_penalty = lax.psum(lax.psum(penalty, 'bus'), 'line')  145 us
    psum x1, waiting for transfers between devices, body(): back = lax.psum(back_part, 'line')  68.3 us
    all_gather x1, waiting for transfers between devices, body(): every_flow = lax.all_gather(line_flows, 'line', axis=1, tiled=True)  49.7 us
    reduce_sum x4, other arithmetic, one_block(): jnp.sum(weight * outage_factors[None, :, :], axis=1)  32.2 us
  transfers between devices with their start and end apart: 5, of which 4 were waited for; matrix products, arithmetic and copies ran while one was open for 0% of the time, Pallas kernels for 0%

profile of v1, /device:TPU:1, one launch (start us, length us, event | category | flops | bytes accessed | tf_op | source)
XLA Modules:
  0.0 1112.7 jit_solution(1569783441586661974)
XLA Ops:
  7.2 0.0 copy-start
  7.2 0.0 copy-start.3
  7.2 0.0 copy-start.2
  7.2 0.0 copy-start.4
  7.2 0.0 copy-start.1
  7.2 0.0 all-reduce.6.cloned.1.call-start
  7.3 1.0 copy-done
  8.2 7.3 fusion.3
  15.5 0.0 all-reduce.6.cloned.1.call-update
  15.5 0.0 all-gather.2.cloned.1.call-start
  15.6 387.3 %all-reduce.6.cloned.1.call-done = f32[64,512]{1,0:T(8,128)} async-done(((f32[64,512]{1,0:T(8,128)}), f32[64,512]{1,0:T(8,128)}) %all-reduce.6.cloned.1.call-update) | async-done | bytes 131088 | tf_op jit(solution)/shard_map/psum | solution.py:21
  402.9 0.0 all-gather.2.cloned.1.call-update
  402.9 0.0 all-reduce.8.cloned.1.call-start
  403.0 0.0 copy-done.3
  403.0 0.0 copy-done.2
  403.0 0.0 copy-done.4
  403.0 0.2 convolution_multiply_fusion
  403.3 49.7 %all-gather.2.cloned.1.call-done = f32[64,4096]{1,0:T(8,128)} async-done(((f32[64,512]{1,0:T(8,128)}), f32[64,4096]{1,0:T(8,128)}) %all-gather.2.cloned.1.call-update) | async-done | bytes 1048592 | tf_op jit(solution)/shard_map/all_gather | solution.py:27
  453.0 1.8 copy.14
  454.8 0.7 gather_fusion
  455.6 0.1 copy.15
  455.7 0.0 copy-done.1
  455.7 40.5 %while.14 = (s32[]{:T(128)}, f32[4,16]{1,0:T(4,128)S(1)}, f32[4,16,512]{2,1,0:T(8,128)}, f32[4,16,256]{2,1,0:T(8,128)}, f32[4,16,512]{2,1,0:T(8,128)}, /*index=5...) while((s32[]{:T(128)}, f32[4,16]{1,0:T(4,128)S(1)}, ...), condition=%wide.region_5.6_spmd, body=%wide.region_1.5_spmd.sunk | while | flops 29478896 | bytes 2491697 | solution.py:52
  455.7 0.8 dynamic-slice_bitcast_fusion.5
  456.5 8.0 multiply_reduce_fusion.4
  464.5 0.6 bitcast_dynamic-update-slice_fusion.4
  465.1 0.6 bitcast_dynamic-update-slice_fusion.5
  465.8 0.8 dynamic-slice_bitcast_fusion.5
  466.6 8.0 multiply_reduce_fusion.4
  474.6 0.6 bitcast_dynamic-update-slice_fusion.4
  475.3 0.6 bitcast_dynamic-update-slice_fusion.5
  475.9 0.8 dynamic-slice_bitcast_fusion.5
  476.7 8.0 multiply_reduce_fusion.4
  484.8 0.6 bitcast_dynamic-update-slice_fusion.4
  485.4 0.6 bitcast_dynamic-update-slice_fusion.5
  486.0 0.8 dynamic-slice_bitcast_fusion.5
  486.8 8.0 multiply_reduce_fusion.4
  494.9 0.6 bitcast_dynamic-update-slice_fusion.4
  495.5 0.6 bitcast_dynamic-update-slice_fusion.5
  496.1 0.0 copy-start.5
  496.1 0.0 all-reduce.8.cloned.1.call-update
  496.2 0.0 all-reduce.10.cloned.1.call-start
  496.2 68.3 %all-reduce.8.cloned.1.call-done = f32[64,256]{1,0:T(8,128)} async-done(((f32[64,256]{1,0:T(8,128)}), f32[64,256]{1,0:T(8,128)}) %all-reduce.8.cloned.1.call-update) | async-done | bytes 65552 | tf_op jit(solution)/shard_map/psum | solution.py:63
  564.5 2.0 convolution_add_fusion
  566.5 0.0 all-reduce.10.cloned.1.call-update
  566.5 0.0 all-reduce.12.cloned.1.call-start
  566.6 385.1 %all-reduce.10.cloned.1.call-done = f32[64,512]{1,0:T(8,128)} async-done(((f32[64,512]{1,0:T(8,128)}), f32[64,512]{1,0:T(8,128)}) %all-reduce.10.cloned.1.call-update) | async-done | bytes 131088 | tf_op jit(solution)/shard_map/psum | solution.py:67
  951.7 5.9 fusion.4
  957.5 0.0 all-reduce.12.cloned.1.call-update
  957.6 0.0 copy-done.5
  957.6 0.6 dynamic-slice
  958.8 0.1 reshape.44
  958.9 101.6 %psum.38 = f32[64]{0:T(128)S(1)} all-reduce(f32[64]{0:T(128)S(1)} %reshape.44), channel_id=1, replica_groups=mesh['line'=8,'bus'=32] {'bus'}, use_global_device_ids=true, to_apply=%region_9.10 | all-reduce | flops 64 | bytes 512 | tf_op jit(solution)/shard_map/psum | solution.py:68
  1060.5 43.6 %psum.39 = f32[64]{0:T(128)S(1)} all-reduce(f32[64]{0:T(128)S(1)} %psum.38), channel_id=1, replica_groups=mesh['line'=8,'bus'=32] {'line'}, use_global_device_ids=true, to_apply=%region_10.11 | all-reduce | flops 64 | bytes 512 | tf_op jit(solution)/shard_map/psum | solution.py:68
  1104.1 0.5 broadcast_multiply_fusion.1
  1104.7 0.0 all-reduce.12.cloned.1.call-done
  1104.7 1.5 constant_dynamic-slice_fusion
  (19 shorter events, 0.3 us)
Async XLA Ops:
  7.2 1.1 copy-start
  7.2 395.8 %copy-start.3 = (s32[256]{0:T(256)S(1)}, s32[256]{0:T(256)}, u32[]{:S(2)}) copy-start(s32[256]{0:T(256)} %param.11) | copy-start | bytes 3076
  7.2 395.8 %copy-start.2 = (s32[4,512]{1,0:T(4,128)S(1)}, s32[4,512]{1,0:T(4,128)}, u32[]{:S(2)}) copy-start(s32[4,512]{1,0:T(4,128)} %param.12) | copy-start | bytes 24580
  7.2 395.8 %copy-start.4 = (s32[64]{0:T(128)S(1)}, s32[64]{0:T(128)}, u32[]{:S(2)}) copy-start(s32[64]{0:T(128)} %param.13) | copy-start | bytes 772
  7.2 448.5 %copy-start.1 = (f32[512,256]{1,0:T(8,128)S(1)}, f32[512,256]{1,0:T(8,128)}, u32[]{:S(2)}) copy-start(f32[512,256]{1,0:T(8,128)} %param.10) | copy-start | bytes 1572868
  7.2 395.6 %all-reduce.6.cloned.1.call-start = ((), (), s32[]{:S(2)}) async-start(), calls=%async_computation | async-start | bytes 262144 | tf_op jit(solution)/shard_map/psum | solution.py:21
  15.5 437.5 %all-gather.2.cloned.1.call-start = ((), (), s32[]{:S(2)}) async-start(), calls=%async_computation.1 | async-start | bytes 1179648 | tf_op jit(solution)/shard_map/all_gather | solution.py:27
  402.9 161.6 %all-reduce.8.cloned.1.call-start = ((), (), s32[]{:S(2)}) async-start(), calls=%async_computation.2 | async-start | bytes 131072 | tf_op jit(solution)/shard_map/psum | solution.py:63
  496.1 461.4 %copy-start.5 = (u32[256]{0:T(256)S(1)}, u32[256]{0:T(256)}, u32[]{:S(2)}) copy-start(u32[256]{0:T(256)} %constant.60) | copy-start | bytes 3076
  496.2 455.5 %all-reduce.10.cloned.1.call-start = ((), (), s32[]{:S(2)}) async-start(), calls=%async_computation.3 | async-start | bytes 262144 | tf_op jit(solution)/shard_map/psum | solution.py:67
  566.5 538.1 %all-reduce.12.cloned.1.call-start = ((), (), s32[]{:S(2)}) async-start(), calls=%async_computation.4 | async-start | bytes 1114112
Sparse Core Ops, SparseCore 0:
  15.6 387.1 all-reduce.5
  404.8 48.1 all-gather.1
  496.3 68.2 all-reduce.7
  567.0 384.6 all-reduce.9
  957.7 83.4 all-reduce.11

commit v2 on v0

--- a/solution.py
+++ b/solution.py
@@ -65,7 +65,7 @@
         back, selector.T, precision=lax.Precision.HIGHEST, preferred_element_type=jnp.float32
     )
     flow_grad, penalty_sum = lax.psum((direct + carried, penalty), "bus")
-    total_penalty = lax.psum(penalty, ("line", "bus"))
+    total_penalty = jnp.sum(lax.all_gather(penalty, ("line", "bus")), axis=0)
     mean_penalty = total_penalty / (LINES * OUTAGES)
     injection_grad = lax.psum_scatter(
         jnp.dot(

time: 1060 us -> 1780 us (1.68)
  blocking collectives: 90.6 us -> 812 us
    all_gather x0 -> x1, blocking collectives: none -> 812 us  [body(): total_penalty = jnp.sum(lax.all_gather(penalty, ('line', 'bus')), axis=0)]
    psum x1 -> x0, blocking collectives: 90.6 us -> none  [body(): total_penalty = lax.psum(penalty, ('line', 'bus'))]
where the time goes in v2:
time: 1780 us
  waiting for transfers between devices  890 us (50%)
  blocking collectives  812 us (46%)
  other arithmetic  33.2 us (2%)
    all_gather x1, blocking collectives, body(): total_penalty = jnp.sum(lax.all_gather(penalty, ('line', 'bus')), axis=0)  812 us
    psum x1, waiting for transfers between devices, body(): line_flows = lax.psum(partial_flows, 'bus')  387 us
    psum x1, waiting for transfers between devices, body(): flow_grad, penalty_sum = lax.psum((direct + carried, penalty), 'bus')  385 us
    psum x1, waiting for transfers between devices, body(): back = lax.psum(back_part, 'line')  68.3 us
    all_gather x1, waiting for transfers between devices, body(): every_flow = lax.all_gather(line_flows, 'line', axis=1, tiled=True)  49.7 us
  transfers between devices with their start and end apart: 5, of which 4 were waited for; matrix products, arithmetic and copies ran while one was open for 0% of the time, Pallas kernels for 0%

profile of v2, /device:TPU:1, one launch (start us, length us, event | category | flops | bytes accessed | tf_op | source)
XLA Modules:
  0.0 1780.1 jit_solution(15492480522946066452)
XLA Ops:
  7.2 0.0 copy-start
  7.2 0.0 copy-start.3
  7.2 0.0 copy-start.2
  7.2 0.0 copy-start.4
  7.2 0.0 copy-start.1
  7.2 0.0 all-reduce.6.cloned.1.call-start
  7.3 1.0 copy-done
  8.2 7.2 fusion.3
  15.5 0.0 all-reduce.6.cloned.1.call-update
  15.5 0.0 all-gather.3.cloned.1.call-start
  15.5 387.3 %all-reduce.6.cloned.1.call-done = f32[64,512]{1,0:T(8,128)} async-done(((f32[64,512]{1,0:T(8,128)}), f32[64,512]{1,0:T(8,128)}) %all-reduce.6.cloned.1.call-update) | async-done | bytes 131088 | tf_op jit(solution)/shard_map/psum | solution.py:21
  402.9 0.0 all-gather.3.cloned.1.call-update
  402.9 0.0 all-reduce.8.cloned.1.call-start
  403.0 0.0 copy-done.3
  403.0 0.0 copy-done.2
  403.0 0.0 copy-done.4
  403.0 0.3 convolution_multiply_fusion
  403.3 49.7 %all-gather.3.cloned.1.call-done = f32[64,4096]{1,0:T(8,128)} async-done(((f32[64,512]{1,0:T(8,128)}), f32[64,4096]{1,0:T(8,128)}) %all-gather.3.cloned.1.call-update) | async-done | bytes 1048592 | tf_op jit(solution)/shard_map/all_gather | solution.py:27
  453.0 1.8 copy.14
  454.8 0.7 gather_fusion
  455.6 0.1 copy.15
  455.7 0.0 copy-done.1
  455.7 40.5 %while.14 = (s32[]{:T(128)}, f32[4,16]{1,0:T(4,128)S(1)}, f32[4,16,512]{2,1,0:T(8,128)}, f32[4,16,256]{2,1,0:T(8,128)}, f32[4,16,512]{2,1,0:T(8,128)}, /*index=5...) while((s32[]{:T(128)}, f32[4,16]{1,0:T(4,128)S(1)}, ...), condition=%wide.region_5.6_spmd, body=%wide.region_1.5_spmd.sunk | while | flops 29478896 | bytes 2491697 | solution.py:52
  455.7 0.8 dynamic-slice_bitcast_fusion.5
  456.5 8.0 multiply_reduce_fusion.4
  464.5 0.6 bitcast_dynamic-update-slice_fusion.4
  465.2 0.6 bitcast_dynamic-update-slice_fusion.5
  465.8 0.8 dynamic-slice_bitcast_fusion.5
  466.6 8.0 multiply_reduce_fusion.4
  474.7 0.6 bitcast_dynamic-update-slice_fusion.4
  475.3 0.6 bitcast_dynamic-update-slice_fusion.5
  475.9 0.8 dynamic-slice_bitcast_fusion.5
  476.7 8.0 multiply_reduce_fusion.4
  484.8 0.6 bitcast_dynamic-update-slice_fusion.4
  485.4 0.6 bitcast_dynamic-update-slice_fusion.5
  486.0 0.8 dynamic-slice_bitcast_fusion.5
  486.8 8.0 multiply_reduce_fusion.4
  494.9 0.6 bitcast_dynamic-update-slice_fusion.4
  495.5 0.6 bitcast_dynamic-update-slice_fusion.5
  496.1 0.0 copy-start.5
  496.1 0.0 all-reduce.8.cloned.1.call-update
  496.2 0.0 all-reduce.10.cloned.1.call-start
  496.2 68.3 %all-reduce.8.cloned.1.call-done = f32[64,256]{1,0:T(8,128)} async-done(((f32[64,256]{1,0:T(8,128)}), f32[64,256]{1,0:T(8,128)}) %all-reduce.8.cloned.1.call-update) | async-done | bytes 65552 | tf_op jit(solution)/shard_map/psum | solution.py:63
  564.5 2.0 convolution_add_fusion
  566.5 0.0 all-reduce.10.cloned.1.call-update
  566.5 0.0 all-reduce.12.cloned.1.call-start
  566.6 385.1 %all-reduce.10.cloned.1.call-done = f32[64,512]{1,0:T(8,128)} async-done(((f32[64,512]{1,0:T(8,128)}), f32[64,512]{1,0:T(8,128)}) %all-reduce.10.cloned.1.call-update) | async-done | bytes 131088 | tf_op jit(solution)/shard_map/psum | solution.py:67
  951.6 5.9 fusion.4
  957.6 0.0 all-reduce.12.cloned.1.call-update
  957.6 0.0 copy-done.5
  957.6 0.6 dynamic-slice
  958.8 0.1 reshape.50
  958.9 812.3 %all-gather = f32[256,1,64]{2,1,0:T(1,128)S(1)} all-gather(f32[1,1,64]{2,1,0:T(1,128)S(1)} %reshape.50), channel_id=1, replica_groups=mesh['line'=8,'bus'=32] {'line','bus'}, dimensions={0}, use_global_device_ids=true | all-gather | bytes 65792 | tf_op jit(solution)/shard_map/all_gather | solution.py:68
  1771.3 0.3 reduce_sum.36
  1771.5 0.5 broadcast_multiply_fusion.1
  1772.1 0.0 all-reduce.12.cloned.1.call-done
  1772.1 1.5 constant_dynamic-slice_fusion
  (19 shorter events, 0.3 us)
Async XLA Ops:
  7.2 1.1 copy-start
  7.2 395.8 %copy-start.3 = (s32[256]{0:T(256)S(1)}, s32[256]{0:T(256)}, u32[]{:S(2)}) copy-start(s32[256]{0:T(256)} %param.11) | copy-start | bytes 3076
  7.2 395.8 %copy-start.2 = (s32[4,512]{1,0:T(4,128)S(1)}, s32[4,512]{1,0:T(4,128)}, u32[]{:S(2)}) copy-start(s32[4,512]{1,0:T(4,128)} %param.12) | copy-start | bytes 24580
  7.2 395.8 %copy-start.4 = (s32[64]{0:T(128)S(1)}, s32[64]{0:T(128)}, u32[]{:S(2)}) copy-start(s32[64]{0:T(128)} %param.13) | copy-start | bytes 772
  7.2 448.4 %copy-start.1 = (f32[512,256]{1,0:T(8,128)S(1)}, f32[512,256]{1,0:T(8,128)}, u32[]{:S(2)}) copy-start(f32[512,256]{1,0:T(8,128)} %param.10) | copy-start | bytes 1572868
  7.2 395.6 %all-reduce.6.cloned.1.call-start = ((), (), s32[]{:S(2)}) async-start(), calls=%async_computation | async-start | bytes 262144 | tf_op jit(solution)/shard_map/psum | solution.py:21
  15.5 437.5 %all-gather.3.cloned.1.call-start = ((), (), s32[]{:S(2)}) async-start(), calls=%async_computation.1 | async-start | bytes 1179648 | tf_op jit(solution)/shard_map/all_gather | solution.py:27
  402.9 161.6 %all-reduce.8.cloned.1.call-start = ((), (), s32[]{:S(2)}) async-start(), calls=%async_computation.2 | async-start | bytes 131072 | tf_op jit(solution)/shard_map/psum | solution.py:63
  496.1 461.5 %copy-start.5 = (u32[256]{0:T(256)S(1)}, u32[256]{0:T(256)}, u32[]{:S(2)}) copy-start(u32[256]{0:T(256)} %constant.61) | copy-start | bytes 3076
  496.2 455.5 %all-reduce.10.cloned.1.call-start = ((), (), s32[]{:S(2)}) async-start(), calls=%async_computation.3 | async-start | bytes 262144 | tf_op jit(solution)/shard_map/psum | solution.py:67
  566.5 1205.5 %all-reduce.12.cloned.1.call-start = ((), (), s32[]{:S(2)}) async-start(), calls=%async_computation.4 | async-start | bytes 1114112
Sparse Core Ops, SparseCore 0:
  15.6 387.1 all-reduce.5
  404.8 48.1 all-gather.2
  496.3 68.2 all-reduce.7
  567.0 384.6 all-reduce.9
  957.7 83.3 all-reduce.11
